TPU v7x, 32 devices: a whole 2x2x4 slice. The times are simulated.
32 devices in a mesh: dp: 2 (over x), slot: 4 (over y, core), hid: 4 (over z).
Axes of the slice: x: 2, y: 2, z: 4, core: 2. Of those that a mesh axis runs over, the one named last changes fastest.
Arguments:
- master_weights: float32 [8, 3, 768, 2048], P('slot', None, 'hid', 'dp'), may hold values from -0.125 to 0.125
- first_moment: float32 [8, 3, 768, 2048], P('slot', None, 'hid', 'dp'), may hold values from -6 to 6
- second_moment: float32 [8, 3, 768, 2048], P('slot', None, 'hid', 'dp'), may hold values from 1 to 100
- tokens_one: bfloat16 [2048, 2048], P('dp'), may hold values from -6 to 6
- grad_out: bfloat16 [2048, 2048], P('dp'), may hold values from -6 to 6
- route_one: int32 [2048, 2], P('dp'), may hold values from 0 to 7, all different within a row
- prob_one: float32 [2048, 2], P('dp'), may hold values from 0.05 to 0.6
- tokens_two: bfloat16 [2048, 2048], P('dp'), may hold values from -6 to 6
- route_two: int32 [2048, 2], P('dp'), may hold values from 0 to 7, all different within a row
- prob_two: float32 [2048, 2], P('dp'), may hold values from 0.05 to 0.6
- old_order: int32 [8], replicated, may hold values from 0 to 7, each once
- new_order: int32 [8], replicated, may hold values from 0 to 7, each once
Outputs:
- moved_master: float32 [8, 3, 768, 2048], P('slot', None, 'hid', 'dp')
- moved_first: float32 [8, 3, 768, 2048], P('slot', None, 'hid', 'dp')
- moved_second: float32 [8, 3, 768, 2048], P('slot', None, 'hid', 'dp')
- next_output: bfloat16 [2048, 2048], P('dp', ('slot', 'hid'))
Inputs may be any that keep to these rules, and one draw needn't show every extreme that they name: `old_order`: lists each of the 8 experts once. `new_order`: lists each of the 8 experts once. `route_one`: each row names 2 different experts. `route_two`: each row names 2 different experts.
All inputs are finite; a program needn't handle non-finite values.
Results may differ from a plain program's by a relative error of at most 0.017.
Values may be sent and summed in bfloat16 or wider, within the bound.
A program may use at most 192 MiB of HBM per device.

v0:
```python
import jax
import jax.numpy as jnp
from jax import lax
from jax.sharding import PartitionSpec as P

learn_rate = 0.001
beta_one = 0.9
beta_two = 0.95
epsilon = 1e-08
decay_rate = 0.1


def rows_by(left, right):
    return lax.dot_general(
        left, right, (((1,), (1,)), ((), ())), preferred_element_type=jnp.float32
    )


def cols_by(left, right):
    return lax.dot_general(
        left, right, (((0,), (0,)), ((), ())), preferred_element_type=jnp.float32
    )


def expert_parts(tokens, grad_out, scaling, weights):
    gate_proj = rows_by(tokens, weights[0])
    up_proj = rows_by(tokens, weights[1])
    logistic = jax.nn.sigmoid(gate_proj)
    swish_gate = gate_proj * logistic
    activated = (swish_gate * up_proj).astype(jnp.bfloat16)
    scaled_grad = (scaling[:, None] * grad_out.astype(jnp.float32)).astype(jnp.bfloat16)
    d_activated = rows_by(scaled_grad, weights[2])
    d_gate = (d_activated * up_proj * logistic * (1.0 + gate_proj * (1.0 - logistic))).astype(
        jnp.bfloat16
    )
    d_up = (d_activated * swish_gate).astype(jnp.bfloat16)
    return (d_gate, d_up, activated, scaled_grad)


def expert_out(tokens, scaling, weights):
    gate_proj = rows_by(tokens, weights[0])
    up_proj = rows_by(tokens, weights[1])
    mixed = (scaling[:, None] * gate_proj * jax.nn.sigmoid(gate_proj) * up_proj).astype(
        jnp.bfloat16
    )
    return jnp.dot(mixed, weights[2], preferred_element_type=jnp.float32)


def adamw_update(master, moment_a, moment_b, grad_sum):
    new_a = beta_one * moment_a + (1.0 - beta_one) * grad_sum
    new_b = beta_two * moment_b + (1.0 - beta_two) * grad_sum * grad_sum
    fixed_a = new_a / (1.0 - beta_one**10)
    fixed_b = new_b / (1.0 - beta_two**10)
    new_master = master - learn_rate * (
        fixed_a / (jnp.sqrt(fixed_b) + epsilon) + decay_rate * master
    )
    return (new_master, new_a, new_b)


def coefficients(routes, probs, expert_ids):
    matches = routes[:, :, None] == expert_ids[None, None, :]
    return jnp.sum(jnp.where(matches, probs[:, :, None], 0.0), axis=1)


def per_device(
    master_weights,
    first_moment,
    second_moment,
    tokens_one,
    grad_out,
    route_one,
    prob_one,
    tokens_two,
    route_two,
    prob_two,
    old_order,
    new_order,
):
    local_count = master_weights.shape[0]
    slot_index = lax.axis_index("slot")
    offset = slot_index * local_count
    held_ids = lax.dynamic_slice_in_dim(old_order, offset, local_count)
    shard_weights = master_weights.astype(jnp.bfloat16)
    full_weights = lax.all_gather(shard_weights, "dp", axis=3, tiled=True)
    scaling_one = coefficients(route_one, prob_one, held_ids)
    parts = [
        expert_parts(tokens_one, grad_out, scaling_one[:, expert], full_weights[expert])
        for expert in range(local_count)
    ]
    gradients = jnp.stack(
        [
            jnp.stack(
                [
                    cols_by(part[0], tokens_one),
                    cols_by(part[1], tokens_one),
                    cols_by(part[2], part[3]),
                ]
            )
            for part in parts
        ]
    )
    owned_grads = lax.psum_scatter(
        gradients.astype(jnp.bfloat16), "dp", scatter_dimension=3, tiled=True
    ).astype(jnp.float32)
    new_master, new_a, new_b = adamw_update(
        master_weights, first_moment, second_moment, owned_grads
    )
    positions = jnp.arange(old_order.shape[0], dtype=jnp.int32)
    source = jnp.sum(
        jnp.where(old_order[None, :] == new_order[:, None], positions[None, :], 0), axis=1
    )
    gathered_states = (
        lax.all_gather(new_master, "slot", axis=0, tiled=True),
        lax.all_gather(new_a, "slot", axis=0, tiled=True),
        lax.all_gather(new_b, "slot", axis=0, tiled=True),
    )
    wanted = lax.dynamic_slice_in_dim(source, offset, local_count)
    moved_states = tuple((jnp.take(state_block, wanted, axis=0) for state_block in gathered_states))
    moved_master, moved_first, moved_second = moved_states
    next_shard = new_master.astype(jnp.bfloat16)
    next_full = lax.all_gather(next_shard, "dp", axis=3, tiled=True)
    scaling_two = coefficients(route_two, prob_two, held_ids)
    partial_value = expert_out(tokens_two, scaling_two[:, 0], next_full[0])
    expert = 1
    partial_value = partial_value + expert_out(
        tokens_two, scaling_two[:, expert], next_full[expert]
    )
    mixed_out = lax.psum_scatter(
        partial_value, ("slot", "hid"), scatter_dimension=1, tiled=True
    ).astype(jnp.bfloat16)
    return (moved_master, moved_first, moved_second, mixed_out)


def solution(mesh):
    in_specs = (
        P("slot", None, "hid", "dp"),
        P("slot", None, "hid", "dp"),
        P("slot", None, "hid", "dp"),
        P("dp", None),
        P("dp", None),
        P("dp", None),
        P("dp", None),
        P("dp", None),
        P("dp", None),
        P("dp", None),
        P(),
        P(),
    )
    out_specs = (
        P("slot", None, "hid", "dp"),
        P("slot", None, "hid", "dp"),
        P("slot", None, "hid", "dp"),
        P("dp", ("slot", "hid")),
    )
    return jax.shard_map(
        per_device, mesh=mesh, in_specs=in_specs, out_specs=out_specs, check_vma=False
    )
```

profile of v0, /device:TPU:0, one launch (start us, length us, event | category | flops | bytes accessed | tf_op | source)
XLA Modules:
  0.0 761.6 jit_solution(9084671307208111710)
XLA Ops:
  7.3 4.1 convert_element_type.49
  11.7 65.2 %all-gather.6.cloned.1.call-done = bf16[2,3,192,2048]{3,2,1,0:T(8,128)(2,1)} async-done(((bf16[2,3,192,1024]{3,2,1,0:T(8,128)(2,1)}), bf16[2,3,192,2048]{3,2,1,0:T(8,128)(2,1)}) %all-gather.6.cloned.1.call-update) | async-done | bytes 4718608 | tf_op jit(solution)/shard_map/all_gather | solution.py:84
  76.9 4.1 fusion.23
  81.0 4.0 fusion.14
  85.1 1.0 fusion.5
  86.1 1.5 fusion.24
  87.7 1.2 fusion.4
  88.9 1.0 copy-done.7
  89.8 1.3 fusion.6
  91.1 1.5 fusion.21
  92.7 1.6 fusion.11
  94.3 1.1 fusion.8
  95.4 1.5 fusion.22
  96.9 1.2 fusion.7
  98.1 1.5 fusion.9
  100.1 2.6 pad_maximum_fusion
  102.8 60.2 %reduce-scatter.3.cloned.1.call-done = bf16[2,3,192,1024]{3,2,1,0:T(8,128)(2,1)} async-done(((bf16[2,3,192,2048]{3,2,1,0:T(8,128)(2,1)}), bf16[2,3,192,1024]{3,2,1,0:T(8,128)(2,1)}) %reduce-scatter.3.cloned.1.call-update) | async-done | bytes 2359312 | tf_op jit(solution)/shard_map/reduce_scatter | solution.py:102
  163.0 11.4 %fusion.59 = (bf16[2,3,192,1024]{3,2,1,0:T(8,128)(2,1)}, f32[2,3,192,1024]{3,2,1,0:T(8,128)}, f32[2,3,192,1024]{3,2,1,0:T(8,128)}, f32[2,3,192,1024]{3,2,1,0:T(8,128)}) fusion(f32[2,3,192,1024]{3,2,1,0:T(8,128)} %param.14, bf16[2,3,192,1024]{3,2,1,0:T(8,128)(2,1)} %reduce-scatter.3.cloned.1.call-done, f32[2,3,192,1024]{3,2,1,0:T(8,128)} %param.15, ...), kind=kLoop, calls=%fused_computation.100 | loop fusion | flops 20054016 | bytes 33030144 | tf_op jit(solution)/shard_map/convert_element_type | solution.py:120
  174.4 62.7 %all-gather.14.cloned.1.call-done = bf16[2,3,192,2048]{3,2,1,0:T(8,128)(2,1)} async-done(((bf16[2,3,192,1024]{3,2,1,0:T(8,128)(2,1)}), bf16[2,3,192,2048]{3,2,1,0:T(8,128)(2,1)}) %all-gather.14.cloned.1.call-update) | async-done | bytes 4718608 | tf_op jit(solution)/shard_map/all_gather | solution.py:121
  237.1 4.1 fusion.20
  241.3 2.7 fusion.19
  243.9 8.7 %fusion.17 = f32[1024,2048]{1,0:T(8,128)} fusion(bf16[1024,2048]{1,0:T(8,128)(2,1)} %param.21, bf16[2,3,192,2048]{3,2,1,0:T(8,128)(2,1)} %all-gather.14.cloned.1.call-done, f32[192,1024]{1,0:T(8,128)S(1)} %fusion.20, f32[1024]{0:T(1024)S(1)} %bitcast.71), kind=kOutput, calls=%fused_computation.36 | convolution fusion | flops 1611988992 | bytes 14946304 | tf_op jit(solution)/shard_map/dot_general | solution.py:46
  252.6 11.2 %convolution_add_fusion = f32[1024,2048]{1,0:T(8,128)} fusion(f32[1024,2048]{1,0:T(8,128)} %fusion.17, bf16[1024,2048]{1,0:T(8,128)(2,1)} %param.21, bf16[2,3,192,2048]{3,2,1,0:T(8,128)(2,1)} %all-gather.14.cloned.1.call-done, f32[192,1024]{1,0:T(8,128)S(1)} %fusion.19, f32[1024]{0:T(1024)S(1)} %bitcast.70), kind=kOutput, calls=%fused_computation.13 | convolution fusion | flops 1614086144 | bytes 23334912 | tf_op jit(solution)/shard_map/dot_general | solution.py:46
  266.1 101.5 %reduce-scatter.5.cloned.1.call-done = f32[1024,128]{1,0:T(8,128)} async-done(((f32[1024,2048]{1,0:T(8,128)}), f32[1024,128]{1,0:T(8,128)}) %reduce-scatter.5.cloned.1.call-update) | async-done | bytes 524304 | tf_op jit(solution)/shard_map/reduce_scatter | solution.py:128
  367.6 1.8 convert_element_type.61
  369.4 119.9 %all-gather.8.cloned.1.call-done = f32[8,3,192,1024]{3,2,1,0:T(8,128)} async-done(((f32[2,3,192,1024]{3,2,1,0:T(8,128)}), f32[8,3,192,1024]{3,2,1,0:T(8,128)}) %all-gather.8.cloned.1.call-update) | async-done | bytes 18874384 | tf_op jit(solution)/shard_map/all_gather | solution.py:113
  489.3 9.7 %gather_fusion = f32[2,3,192,1024]{3,2,1,0:T(8,128)} fusion(f32[8,3,192,1024]{3,2,1,0:T(8,128)} %all-gather.8.cloned.1.call-done, s32[1024]{0:T(1024)S(1)} %pad_clamp_fusion), kind=kCustom, calls=%fused_computation.clone | custom fusion | bytes 9437192 | tf_op jit(solution)/shard_map/jit(_take)/gather | solution.py:118
  499.0 112.4 %all-gather.10.cloned.1.call-done = f32[8,3,192,1024]{3,2,1,0:T(8,128)} async-done(((f32[2,3,192,1024]{3,2,1,0:T(8,128)}), f32[8,3,192,1024]{3,2,1,0:T(8,128)}) %all-gather.10.cloned.1.call-update) | async-done | bytes 18874384 | tf_op jit(solution)/shard_map/all_gather | solution.py:114
  611.3 9.7 %gather_fusion.1 = f32[2,3,192,1024]{3,2,1,0:T(8,128)} fusion(f32[8,3,192,1024]{3,2,1,0:T(8,128)} %all-gather.10.cloned.1.call-done, s32[1024]{0:T(1024)S(1)} %pad_clamp_fusion), kind=kCustom, calls=%fused_computation.1.clone | custom fusion | bytes 9437192 | tf_op jit(solution)/shard_map/jit(_take)/gather | solution.py:118
  621.0 112.5 %all-gather.12.cloned.1.call-done = f32[8,3,192,1024]{3,2,1,0:T(8,128)} async-done(((f32[2,3,192,1024]{3,2,1,0:T(8,128)}), f32[8,3,192,1024]{3,2,1,0:T(8,128)}) %all-gather.12.cloned.1.call-update) | async-done | bytes 18874384 | tf_op jit(solution)/shard_map/all_gather | solution.py:115
  733.5 9.4 %gather_fusion.2 = f32[2,3,192,1024]{3,2,1,0:T(8,128)} fusion(f32[8,3,192,1024]{3,2,1,0:T(8,128)} %all-gather.12.cloned.1.call-done, s32[1024]{0:T(1024)S(1)} %pad_clamp_fusion), kind=kCustom, calls=%fused_computation.2.clone | custom fusion | bytes 9437192 | tf_op jit(solution)/shard_map/jit(_take)/gather | solution.py:118
  742.9 11.9 %broadcast_select_fusion = (f32[2,3,192,1024]{3,2,1,0:T(8,128)}, f32[2,3,192,1024]{3,2,1,0:T(8,128)}, f32[2,3,192,1024]{3,2,1,0:T(8,128)}) fusion(f32[2,3,192,1024]{3,2,1,0:T(8,128)} %gather_fusion.2, pred[2]{0:T(512)(128)(4,1)S(1)} %get-tuple-element.11, f32[2,3,192,1024]{3,2,1,0:T(8,128)} %gather_fusion.1, f32[2,3,192,1024]{3,2,1,0:T(8,128)} %gather_fusion), kind=kLoop, calls=%fused_computation.28 | loop fusion | flops 3538944 | bytes 28311554 | tf_op jit(solution)/shard_map/jit(_take)/select_n | solution.py:118
  (41 shorter events, 3.1 us)
Async XLA Ops:
  7.2 4.3 copy-start.8
  7.2 4.4 copy-start.4
  7.2 4.4 copy-start.3
  7.2 4.4 copy-start.2
  7.2 4.4 copy-start.1
  7.2 69.7 %all-gather.6.cloned.1.call-start = ((), (), s32[]{:S(2)}) async-start(), calls=%async_computation.2 | async-start | bytes 7077888 | tf_op jit(solution)/shard_map/all_gather | solution.py:84
  11.4 151.6 %reduce-scatter.3.cloned.1.call-start = ((), (), s32[]{:S(2)}) async-start(), calls=%async_computation.3 | async-start | bytes 7077888 | tf_op jit(solution)/shard_map/reduce_scatter | solution.py:102
  76.9 4.1 copy-start.5
  81.0 4.1 copy-start.6
  87.7 2.2 copy-start.7
  102.7 134.4 %all-gather.14.cloned.1.call-start = ((), (), s32[]{:S(2)}) async-start(), calls=%async_computation.7 | async-start | bytes 7077888 | tf_op jit(solution)/shard_map/all_gather | solution.py:121
  174.3 193.3 %reduce-scatter.5.cloned.1.call-start = ((), (), s32[]{:S(2)}) async-start(), calls=%async_computation.8 | async-start | bytes 8912896 | tf_op jit(solution)/shard_map/reduce_scatter | solution.py:128
  237.1 4.1 copy-start
  263.9 225.4 %all-gather.8.cloned.1.call-start = ((), (), s32[]{:S(2)}) async-start(), calls=%async_computation.4 | async-start | bytes 23592960 | tf_op jit(solution)/shard_map/all_gather | solution.py:113
  264.5 346.9 %all-gather.10.cloned.1.call-start = ((), (), s32[]{:S(2)}) async-start(), calls=%async_computation.5 | async-start | bytes 23592960 | tf_op jit(solution)/shard_map/all_gather | solution.py:114
  264.5 1.3 copy-start.9
  265.1 468.5 %all-gather.12.cloned.1.call-start = ((), (), s32[]{:S(2)}) async-start(), calls=%async_computation.6 | async-start | bytes 23592960 | tf_op jit(solution)/shard_map/all_gather | solution.py:115
Sparse Core Ops, SparseCore 0:
  11.5 65.3 all-gather.5
  102.9 60.0 reduce-scatter.2
  174.5 62.6 all-gather.13
  264.0 103.5 reduce-scatter.4
  369.6 119.6 all-gather.7
  491.3 119.9 all-gather.9
  613.5 119.9 all-gather.11
where the time goes:
time: 762 us
  waiting for transfers between devices  636 us (83%)
  matrix products  48.3 us (6%)
  other arithmetic  32.6 us (4%)
  local copies, waits for them, and re-layouts  29.8 us (4%)
  between operations  14.4 us (2%)
    all_gather x1, waiting for transfers between devices, per_device(): lax.all_gather(new_master, 'slot', axis=0, tiled=True)  120 us
    all_gather x1, waiting for transfers between devices, per_device(): lax.all_gather(new_b, 'slot', axis=0, tiled=True)  113 us
    all_gather x1, waiting for transfers between devices, per_device(): lax.all_gather(new_a, 'slot', axis=0, tiled=True)  112 us
    reduce_scatter x1, waiting for transfers between devices, per_device(): lax.psum_scatter(partial_value, ('slot', 'hid'), scatter_dimension=1, til...  102 us
    all_gather x1, waiting for transfers between devices, per_device(): full_weights = lax.all_gather(shard_weights, 'dp', axis=3, tiled=True)  65.2 us
    all_gather x1, waiting for transfers between devices, per_device(): next_full = lax.all_gather(next_shard, 'dp', axis=3, tiled=True)  62.7 us
    reduce_scatter x1, waiting for transfers between devices, per_device(): lax.psum_scatter(gradients.astype(jnp.bfloat16), 'dp', scatter_dimension=...  60.2 us
    gather x3, local copies, waits for them, and re-layouts, per_device(): jnp.take(state_block, wanted, axis=0)  28.7 us
  transfers between devices with their start and end apart: 7, of which 7 were waited for; matrix products, arithmetic and copies ran while one was open for 3% of the time, Pallas kernels for 0%

commit v1 on v0

--- a/solution.py
+++ b/solution.py
@@ -8,6 +8,27 @@
 beta_two = 0.95
 epsilon = 1e-08
 decay_rate = 0.1
+
+
+def collect(shard, axis, dim):
+    devices, here, rows = (lax.axis_size(axis), lax.axis_index(axis), shard.shape[dim])
+    ahead = [(i, (i + 1) % devices) for i in range(devices)]
+    backward = [(i, (i - 1) % devices) for i in range(devices)]
+    result = jnp.zeros((*shard.shape[:dim], devices * rows, *shard.shape[dim + 1 :]), shard.dtype)
+    result = lax.dynamic_update_slice_in_dim(result, shard, here * rows, axis=dim)
+    from_left = from_right = shard
+    halfway = devices // 2
+    for lap in range(1, halfway + 1):
+        from_left = lax.ppermute(from_left, axis, ahead)
+        result = lax.dynamic_update_slice_in_dim(
+            result, from_left, (here - lap) % devices * rows, axis=dim
+        )
+        if lap < devices - halfway:
+            from_right = lax.ppermute(from_right, axis, backward)
+            result = lax.dynamic_update_slice_in_dim(
+                result, from_right, (here + lap) % devices * rows, axis=dim
+            )
+    return result
 
 
 def rows_by(left, right):
@@ -112,7 +133,7 @@
     gathered_states = (
         lax.all_gather(new_master, "slot", axis=0, tiled=True),
         lax.all_gather(new_a, "slot", axis=0, tiled=True),
-        lax.all_gather(new_b, "slot", axis=0, tiled=True),
+        collect(new_b, "slot", 0),
     )
     wanted = lax.dynamic_slice_in_dim(source, offset, local_count)
     moved_states = tuple((jnp.take(state_block, wanted, axis=0) for state_block in gathered_states))

time: 762 us -> 705 us (0.925)
  waiting for transfers between devices: 636 us -> 546 us
  local copies, waits for them, and re-layouts: 29.8 us -> 60.5 us
    ppermute x0 -> x3, waiting for transfers between devices: none -> 241 us  [the longest x2 241 us: collect(): from_left = lax.ppermute(from_left, axis, ahead)]
    all_gather x1, waiting for transfers between devices: 120 us -> 2.03 us  [per_device(): lax.all_gather(new_master, 'slot', axis=0, tiled=True)]
    all_gather x1 -> x0, waiting for transfers between devices: 113 us -> none  [per_device(): lax.all_gather(new_b, 'slot', axis=0, tiled=True)]
    reduce_scatter x1, waiting for transfers between devices: 102 us -> 0.01 us  [per_device(): lax.psum_scatter(partial_value, ('slot', 'hid'), scatter_dimension=1, til...]
    dynamic_update_slice x0 -> x4, local copies, waits for them, and re-layouts: none -> 18.1 us  [the longest x2 10.3 us: collect(): lax.dynamic_update_slice_in_dim(result, from_left, (here - lap) % devices...]
    broadcast_in_dim x0 -> x1, local copies, waits for them, and re-layouts: none -> 13.1 us  [collect(): jnp.zeros((*shard.shape[:dim], devices * rows, *shard.shape[dim + 1:]), s...]
  transfers between devices with their start and end apart: 7 -> 9, of which waited for: 7 -> 7; matrix products, arithmetic and copies ran while one was open for 3% -> 7% of each run, Pallas kernels for 0% -> 0%
where the time goes in v1:
time: 705 us; the launch traced here: 704 us
  waiting for transfers between devices  546 us (77%)
  local copies, waits for them, and re-layouts  60.5 us (9%)
  matrix products  48.2 us (7%)
  other arithmetic  32.6 us (5%)
  between operations  14.4 us (2%)
    ppermute x2, waiting for transfers between devices, collect(): from_left = lax.ppermute(from_left, axis, ahead)  241 us
    all_gather x1, waiting for transfers between devices, per_device(): lax.all_gather(new_a, 'slot', axis=0, tiled=True)  114 us
    all_gather x1, waiting for transfers between devices, per_device(): full_weights = lax.all_gather(shard_weights, 'dp', axis=3, tiled=True)  65.2 us
    all_gather x1, waiting for transfers between devices, per_device(): next_full = lax.all_gather(next_shard, 'dp', axis=3, tiled=True)  62.7 us
    reduce_scatter x1, waiting for transfers between devices, per_device(): lax.psum_scatter(gradients.astype(jnp.bfloat16), 'dp', scatter_dimension=...  60.2 us
    gather x3, local copies, waits for them, and re-layouts, per_device(): jnp.take(state_block, wanted, axis=0)  28.2 us
    dot_general x8, matrix products, rows_by(): lax.dot_general(left, right, (((1,), (1,)), ((), ())), preferred_element_...  21.1 us
    dot_general x2, matrix products, expert_out(): return jnp.dot(mixed, weights[2], preferred_element_type=jnp.float32)  19.9 us
  transfers between devices with their start and end apart: 9, of which 7 were waited for; matrix products, arithmetic and copies ran while one was open for 7% of the time, Pallas kernels for 0%

profile of v1, /device:TPU:0, one launch (start us, length us, event | category | flops | bytes accessed | tf_op | source)
XLA Modules:
  0.0 704.0 jit_solution(3758802639195248260)
XLA Ops:
  7.3 4.1 convert_element_type.49
  11.7 65.2 %all-gather.5.cloned.1.call-done = bf16[2,3,192,2048]{3,2,1,0:T(8,128)(2,1)} async-done(((bf16[2,3,192,1024]{3,2,1,0:T(8,128)(2,1)}), bf16[2,3,192,2048]{3,2,1,0:T(8,128)(2,1)}) %all-gather.5.cloned.1.call-update) | async-done | bytes 4718608 | tf_op jit(solution)/shard_map/all_gather | solution.py:105
  76.9 4.1 fusion.23
  81.0 4.0 fusion.14
  86.1 1.5 fusion.24
  91.1 1.5 fusion.21
  92.7 1.6 fusion.11
  95.4 1.5 fusion.22
  98.1 1.5 fusion.9
  100.1 2.6 pad_maximum_fusion
  102.8 60.2 %reduce-scatter.3.cloned.1.call-done = bf16[2,3,192,1024]{3,2,1,0:T(8,128)(2,1)} async-done(((bf16[2,3,192,2048]{3,2,1,0:T(8,128)(2,1)}), bf16[2,3,192,1024]{3,2,1,0:T(8,128)(2,1)}) %reduce-scatter.3.cloned.1.call-update) | async-done | bytes 2359312 | tf_op jit(solution)/shard_map/reduce_scatter | solution.py:123
  163.0 11.4 %fusion.59 = (bf16[2,3,192,1024]{3,2,1,0:T(8,128)(2,1)}, f32[2,3,192,1024]{3,2,1,0:T(8,128)}, f32[2,3,192,1024]{3,2,1,0:T(8,128)}, f32[2,3,192,1024]{3,2,1,0:T(8,128)}) fusion(f32[2,3,192,1024]{3,2,1,0:T(8,128)} %param.14, bf16[2,3,192,1024]{3,2,1,0:T(8,128)(2,1)} %reduce-scatter.3.cloned.1.call-done, f32[2,3,192,1024]{3,2,1,0:T(8,128)} %param.15, ...), kind=kLoop, calls=%fused_computation.104 | loop fusion | flops 20054016 | bytes 33030144 | tf_op jit(solution)/shard_map/convert_element_type | solution.py:141
  174.4 62.7 %all-gather.11.cloned.1.call-done = bf16[2,3,192,2048]{3,2,1,0:T(8,128)(2,1)} async-done(((bf16[2,3,192,1024]{3,2,1,0:T(8,128)(2,1)}), bf16[2,3,192,2048]{3,2,1,0:T(8,128)(2,1)}) %all-gather.11.cloned.1.call-update) | async-done | bytes 4718608 | tf_op jit(solution)/shard_map/all_gather | solution.py:142
  237.1 4.1 fusion.20
  241.3 2.7 fusion.19
  243.9 8.7 %fusion.17 = f32[1024,2048]{1,0:T(8,128)} fusion(bf16[1024,2048]{1,0:T(8,128)(2,1)} %param.21, bf16[2,3,192,2048]{3,2,1,0:T(8,128)(2,1)} %all-gather.11.cloned.1.call-done, f32[192,1024]{1,0:T(8,128)S(1)} %fusion.20, f32[1024]{0:T(1024)S(1)} %bitcast.73), kind=kOutput, calls=%fused_computation.36 | convolution fusion | flops 1611988992 | bytes 14946304 | tf_op jit(solution)/shard_map/dot_general | solution.py:67
  252.6 11.2 %convolution_add_fusion = f32[1024,2048]{1,0:T(8,128)} fusion(f32[1024,2048]{1,0:T(8,128)} %fusion.17, bf16[1024,2048]{1,0:T(8,128)(2,1)} %param.21, bf16[2,3,192,2048]{3,2,1,0:T(8,128)(2,1)} %all-gather.11.cloned.1.call-done, f32[192,1024]{1,0:T(8,128)S(1)} %fusion.19, f32[1024]{0:T(1024)S(1)} %bitcast.72), kind=kOutput, calls=%fused_computation.13 | convolution fusion | flops 1614086144 | bytes 23334912 | tf_op jit(solution)/shard_map/dot_general | solution.py:67
  265.1 1.7 collective-permute-start.1
  266.8 129.0 %collective-permute-done = f32[2,3,192,1024]{3,2,1,0:T(8,128)} collective-permute-done((f32[2,3,192,1024]{3,2,1,0:T(8,128)}, f32[2,3,192,1024]{3,2,1,0:T(8,128)}, u32[]{:S(2)}, u32[]{:S(2)}) %collective-permute-start) | collective-permute-done | bytes 4718624 | tf_op jit(solution)/shard_map/ppermute | solution.py:22
  396.1 13.1 %broadcast_in_dim.55 = f32[8,3,192,1024]{3,2,1,0:T(8,128)} broadcast(f32[]{:T(128)} %constant.56.clone.1), dimensions={} | broadcast | bytes 18874372 | tf_op jit(solution)/shard_map/broadcast_in_dim | solution.py:17
  409.2 2.5 constant_dynamic-update-slice_fusion.3
  411.7 5.2 constant_dynamic-update-slice_fusion.2
  416.9 5.3 constant_dynamic-update-slice_fusion.1
  422.2 112.4 %collective-permute-done.2 = f32[2,3,192,1024]{3,2,1,0:T(8,128)} collective-permute-done((f32[2,3,192,1024]{3,2,1,0:T(8,128)}, f32[2,3,192,1024]{3,2,1,0:T(8,128)}, u32[]{:S(2)}, u32[]{:S(2)}) %collective-permute-start.2) | collective-permute-done | bytes 4718624 | tf_op jit(solution)/shard_map/ppermute | solution.py:22
  534.6 5.1 constant_dynamic-update-slice_fusion
  539.8 9.4 %gather_fusion.2 = f32[2,3,192,1024]{3,2,1,0:T(8,128)} fusion(f32[8,3,192,1024]{3,2,1,0:T(8,128)} %constant_dynamic-update-slice_fusion, s32[1024]{0:T(1024)S(1)} %pad_clamp_fusion), kind=kCustom, calls=%fused_computation.2.clone | custom fusion | bytes 9437192 | tf_op jit(solution)/shard_map/jit(_take)/gather | solution.py:139
  549.2 1.8 convert_element_type.61
  550.9 2.0 all-gather.7.cloned.1.call-done
  553.0 9.4 %gather_fusion = f32[2,3,192,1024]{3,2,1,0:T(8,128)} fusion(f32[8,3,192,1024]{3,2,1,0:T(8,128)} %all-gather.7.cloned.1.call-done, s32[1024]{0:T(1024)S(1)} %pad_clamp_fusion), kind=kCustom, calls=%fused_computation.clone | custom fusion | bytes 9437192 | tf_op jit(solution)/shard_map/jit(_take)/gather | solution.py:139
  562.3 113.6 %all-gather.9.cloned.1.call-done = f32[8,3,192,1024]{3,2,1,0:T(8,128)} async-done(((f32[2,3,192,1024]{3,2,1,0:T(8,128)}), f32[8,3,192,1024]{3,2,1,0:T(8,128)}) %all-gather.9.cloned.1.call-update) | async-done | bytes 18874384 | tf_op jit(solution)/shard_map/all_gather | solution.py:135
  675.9 9.4 %gather_fusion.1 = f32[2,3,192,1024]{3,2,1,0:T(8,128)} fusion(f32[8,3,192,1024]{3,2,1,0:T(8,128)} %all-gather.9.cloned.1.call-done, s32[1024]{0:T(1024)S(1)} %pad_clamp_fusion), kind=kCustom, calls=%fused_computation.1.clone | custom fusion | bytes 9437192 | tf_op jit(solution)/shard_map/jit(_take)/gather | solution.py:139
  685.3 11.9 %broadcast_select_fusion = (f32[2,3,192,1024]{3,2,1,0:T(8,128)}, f32[2,3,192,1024]{3,2,1,0:T(8,128)}, f32[2,3,192,1024]{3,2,1,0:T(8,128)}) fusion(f32[2,3,192,1024]{3,2,1,0:T(8,128)} %gather_fusion.2, pred[2]{0:T(512)(128)(4,1)S(1)} %get-tuple-element.11, f32[2,3,192,1024]{3,2,1,0:T(8,128)} %gather_fusion.1, f32[2,3,192,1024]{3,2,1,0:T(8,128)} %gather_fusion), kind=kLoop, calls=%fused_computation.28 | loop fusion | flops 3538944 | bytes 28311554 | tf_op jit(solution)/shard_map/jit(_take)/select_n | solution.py:139
  (54 shorter events, 9.2 us)
Async XLA Ops:
  7.2 4.3 copy-start.8
  7.2 4.4 copy-start.4
  7.2 4.4 copy-start.3
  7.2 4.4 copy-start.2
  7.2 4.4 copy-start.1
  7.2 69.7 %all-gather.5.cloned.1.call-start = ((), (), s32[]{:S(2)}) async-start(), calls=%async_computation.2 | async-start | bytes 7077888 | tf_op jit(solution)/shard_map/all_gather | solution.py:105
  11.4 151.6 %reduce-scatter.3.cloned.1.call-start = ((), (), s32[]{:S(2)}) async-start(), calls=%async_computation.3 | async-start | bytes 7077888 | tf_op jit(solution)/shard_map/reduce_scatter | solution.py:123
  76.9 4.1 copy-start.5
  81.0 4.1 copy-start.6
  87.7 2.2 copy-start.7
  102.8 134.4 %all-gather.11.cloned.1.call-start = ((), (), s32[]{:S(2)}) async-start(), calls=%async_computation.6 | async-start | bytes 7077888 | tf_op jit(solution)/shard_map/all_gather | solution.py:142
  174.4 374.8 %reduce-scatter.5.cloned.1.call-start = ((), (), s32[]{:S(2)}) async-start(), calls=%async_computation.7 | async-start | bytes 8912896 | tf_op jit(solution)/shard_map/reduce_scatter | solution.py:149
  237.1 4.1 copy-start
  263.9 289.1 %all-gather.7.cloned.1.call-start = ((), (), s32[]{:S(2)}) async-start(), calls=%async_computation.4 | async-start | bytes 23592960 | tf_op jit(solution)/shard_map/all_gather | solution.py:134
  263.9 132.0 %copy-start.9 = (s32[8]{0:T(128)S(1)}, s32[8]{0:T(128)}, u32[]{:S(2)}) copy-start(s32[8]{0:T(128)} %param.25) | copy-start | bytes 100
  264.5 411.5 %all-gather.9.cloned.1.call-start = ((), (), s32[]{:S(2)}) async-start(), calls=%async_computation.5 | async-start | bytes 23592960 | tf_op jit(solution)/shard_map/all_gather | solution.py:135
  264.5 144.7 %slice-start = ((s8[4718592]{0:T(1024)(128)(4,1)}), s8[524288]{0:T(1024)(128)(4,1)S(1)}, s32[]{:S(2)}) async-start(s8[4718592]{0:T(1024)(128)(4,1)} %bitcast.70), calls=%async_computation.8 | async-start | bytes 1048576
  265.0 130.8 %collective-permute-start = (f32[2,3,192,1024]{3,2,1,0:T(8,128)}, f32[2,3,192,1024]{3,2,1,0:T(8,128)}, u32[]{:S(2)}, u32[]{:S(2)}) collective-permute-start(f32[2,3,192,1024]{3,2,1,0:T(8,128)} %get-tuple-element.10), channel_id=1, source_target_pairs={{0,4},{4,8},{8,12},{12,0},{1,5},{5,9},{9,13},{13,1},{2,6},{6,10},{... | collective-permute-start | bytes 14155784 | tf_op jit(solution)/shard_map/ppermute | solution.py:22
  265.1 151.8 %collective-permute-start.1 = (f32[2,3,192,1024]{3,2,1,0:T(8,128)}, f32[2,3,192,1024]{3,2,1,0:T(8,128)}, u32[]{:S(2)}, u32[]{:S(2)}) collective-permute-start(f32[2,3,192,1024]{3,2,1,0:T(8,128)} %get-tuple-element.10), channel_id=1, source_target_pairs={{0,12},{4,0},{8,4},{12,8},{1,13},{5,1},{9,5},{13,9},{2,14},{6,2},{... | collective-permute-start | bytes 14155784 | tf_op jit(solution)/shard_map/ppermute | solution.py:27
  395.8 138.8 %collective-permute-start.2 = (f32[2,3,192,1024]{3,2,1,0:T(8,128)}, f32[2,3,192,1024]{3,2,1,0:T(8,128)}, u32[]{:S(2)}, u32[]{:S(2)}) collective-permute-start(f32[2,3,192,1024]{3,2,1,0:T(8,128)} %collective-permute-done), channel_id=1, source_target_pairs={{0,4},{4,8},{8,12},{12,0},{1,5},{5,9},{9,13},{13,1},{2,6},{6,10},{... | collective-permute-start | bytes 14155784 | tf_op jit(solution)/shard_map/ppermute | solution.py:22
  396.1 13.1 %slice-start.1 = ((s8[4718592]{0:T(1024)(128)(4,1)}), s8[4194304]{0:T(1024)(128)(4,1)S(1)}, s32[]{:S(2)}) async-start(s8[4718592]{0:T(1024)(128)(4,1)} %bitcast.70), calls=%async_computation.9 | async-start | bytes 8388608
Sparse Core Ops, SparseCore 0:
  11.5 65.3 all-gather.4
  102.9 60.0 reduce-scatter.2
  174.5 62.6 all-gather.10
  264.0 126.0 reduce-scatter.4
  392.1 160.8 all-gather.6
  555.0 120.9 all-gather.8
